TPU v7x, 512 devices: a whole 4x8x8 slice. The times are simulated.
512 devices in a mesh: src: 16 (over y, core), tgt: 32 (over x, z).
Axes of the slice: x: 4, y: 8, z: 8, core: 2. Of those that a mesh axis runs over, the one named last changes fastest.
Arguments:
- noise: float32 [16384, 384], P(('src', 'tgt')), may hold values from -16 to 16
- data: float32 [32768, 384], P('tgt', 'src'), may hold values from -6 to 6
Outputs:
- velocity: float32 [16384, 384], P(('src', 'tgt'))
- target_potential: float32 [32768], P('tgt')
All inputs are finite; a program needn't handle non-finite values.
Results may differ from a plain program's by a relative error of at most 0.0003.
Values sent between devices are 32-bit elements; how exact they have to be, the bound alone decides.
No kernel may reach another device: no remote copies, remote signals or barrier semaphores. Data moves between devices by JAX's collectives and lax.ppermute only.
A program may use at most 64 MiB of HBM per device.

v0:
```python
import math
import jax
import jax.numpy as jnp
from jax import lax
from jax.sharding import PartitionSpec as P

ITERS = 3
EPS = 0.05


def spread(value, axis):
    count = lax.axis_size(axis)
    return lax.all_to_all(jnp.broadcast_to(value[None], (count,) + value.shape), axis, 0, 0)


def total_over(local_sum, axis):
    tiles = local_sum.reshape(-1, 128)
    return jnp.sum(spread(tiles, axis), axis=0).reshape(local_sum.shape)


def lse_over(local_top, local_sum, axis):
    tiles = spread((local_top + jnp.log(local_sum)).reshape(-1, 128), axis)
    top = jnp.max(tiles, axis=0)
    merged = top + jnp.log(jnp.sum(jnp.exp(tiles - top[None]), axis=0))
    return merged.reshape(local_top.shape)


def per_device(noise, data):
    target_rows = lax.all_gather(data, "src", axis=1, tiled=True)
    own_rows, feat_width = noise.shape
    source_rows = spread(noise, "tgt").reshape(-1, feat_width)
    src_total = source_rows.shape[0] * lax.axis_size("src")
    tgt_total = target_rows.shape[0] * lax.axis_size("tgt")
    source_sq = jnp.sum(source_rows * source_rows, axis=1)
    target_sq = jnp.sum(target_rows * target_rows, axis=1)
    cross = jnp.dot(
        source_rows,
        target_rows.T,
        precision=lax.Precision.HIGHEST,
        preferred_element_type=jnp.float32,
    )
    gain = (2.0 * cross - source_sq[:, None] - target_sq[None, :]) / (feat_width * EPS)
    log_src, log_tgt = (math.log(src_total), math.log(tgt_total))
    top = jnp.max(gain, axis=1)
    f_pot = -(log_src + lse_over(top, jnp.sum(jnp.exp(gain - top[:, None]), axis=1), "tgt"))
    z_tile = f_pot[:, None] + gain
    top = jnp.max(z_tile, axis=0)
    g_pot = -(log_tgt + lse_over(top, jnp.sum(jnp.exp(z_tile - top[None, :]), axis=0), "src"))
    for step_index in range(1, ITERS):
        mass = jnp.sum(jnp.exp(f_pot[:, None] + gain + g_pot[None, :]), axis=1)
        f_pot = f_pot - (log_src + jnp.log(total_over(mass, "tgt")))
        mass = jnp.sum(jnp.exp(f_pot[:, None] + gain + g_pot[None, :]), axis=0)
        g_pot = g_pot - (log_tgt + jnp.log(total_over(mass, "src")))
    plan = jnp.exp(f_pot[:, None] + gain + g_pot[None, :])
    mass = jnp.sum(plan, axis=1)
    part = jnp.dot(
        plan, target_rows, precision=lax.Precision.HIGHEST, preferred_element_type=jnp.float32
    )
    count = lax.axis_size("tgt")
    part = lax.all_to_all(part.reshape(count, own_rows, feat_width), "tgt", 0, 0)
    mass = lax.all_to_all(mass.reshape(count, own_rows), "tgt", 0, 0)
    bary = jnp.sum(part, axis=0) / jnp.sum(mass, axis=0)[:, None]
    return (bary - noise, EPS * g_pot)


def solution(mesh):
    placed = (P(("src", "tgt"), None), P("tgt", "src"))
    return jax.shard_map(
        per_device,
        mesh=mesh,
        in_specs=placed,
        out_specs=(P(("src", "tgt"), None), P("tgt")),
        check_vma=False,
    )
```

profile of v0, /device:TPU:8, one launch (start us, length us, event | category | flops | bytes accessed | tf_op | source)
XLA Modules:
  0.0 251.7 jit_solution(776631761340296787)
XLA Ops:
  7.9 2.1 broadcast_in_dim.22
  10.0 13.2 %all-to-all-start = ((f32[32,32,384]{2,1,0:T(8,128)}), f32[32,32,384]{2,1,0:T(8,128)S(1)}, u32[]{:S(2)}, u32[]{:S(2)}) async-start(f32[32,32,384]{2,1,0:T(8,128)} %broadcast_in_dim.22), calls=%async_computation | async-start | bytes 3145728 | tf_op jit(solution)/shard_map/all_to_all | solution.py:13
  23.2 32.4 %all-gather.2.cloned.1.call-done = f32[1024,384]{0,1:T(8,128)} async-done(((f32[1024,24]{0,1:T(8,128)}), f32[1024,384]{0,1:T(8,128)}) %all-gather.2.cloned.1.call-update) | async-done | bytes 1572880 | tf_op jit(solution)/shard_map/all_gather | solution.py:29
  55.6 1.5 multiply_reduce_fusion
  57.1 5.4 %all-to-all-done = f32[32,32,384]{2,1,0:T(8,128)S(1)} async-done(((f32[32,32,384]{2,1,0:T(8,128)}), f32[32,32,384]{2,1,0:T(8,128)S(1)}, u32[]{:S(2)}, u32[]{:S(2)}) %all-to-all-start) | async-done | bytes 1572896 | tf_op jit(solution)/shard_map/all_to_all | solution.py:13
  62.8 8.9 %fusion.4 = (f32[1024]{0:T(1024)S(1)}, f32[1024,1024]{0,1:T(8,128)S(1)}) fusion(f32[1024]{0:T(1024)S(1)} %multiply_reduce_fusion, f32[1024]{0:T(1024)S(1)} %sub.87, f32[1024,384]{1,0:T(8,128)S(1)} %bitcast.27, f32[1024,384]{0,1:T(8,128)} %all-gather.2.cloned.1.call-done), kind=kOutput, calls=%fused_computation.27 | convolution fusion | flops 4837080064 | bytes 7352320 | tf_op jit(solution)/shard_map/dot_general | solution.py:36
  71.7 1.9 copy-done
  74.3 15.8 %all_to_all.49 = f32[32,8,128]{2,1,0:T(8,128)S(1)} all-to-all(f32[32,8,128]{2,1,0:T(8,128)S(1)} %broadcast_in_dim.23), channel_id=1, replica_groups=mesh['src'=16,'tgt'=32] {'tgt'}, dimensions={0} | all-to-all | bytes 262144 | tf_op jit(solution)/shard_map/all_to_all | solution.py:13
  90.2 2.7 %add_reduce_fusion = f32[1024]{0:T(1024)S(1)} fusion(f32[1024,1024]{0,1:T(8,128)} %copy-done, f32[1024]{0:T(1024)S(1)} %negate_bitcast_fusion.1), kind=kLoop, calls=%fused_computation.8 | loop fusion | flops 2096128 | bytes 4202496 | tf_op jit(solution)/shard_map/reduce_max | solution.py:47
  93.5 0.9 exponential_reduce_fusion.4
  94.5 13.9 %all_to_all.50 = f32[16,8,128]{2,1,0:T(8,128)S(1)} all-to-all(f32[16,8,128]{2,1,0:T(8,128)S(1)} %broadcast_in_dim.24), channel_id=1, replica_groups=mesh['src'=16,'tgt'=32] {'src'}, dimensions={0} | all-to-all | bytes 131072 | tf_op jit(solution)/shard_map/all_to_all | solution.py:13
  108.5 2.9 %exponential_reduce_fusion.3 = f32[1024]{0:T(1024)S(1)} fusion(f32[1024,1024]{0,1:T(8,128)} %copy-done, f32[1024]{0:T(1024)S(1)} %negate_bitcast_fusion, f32[1024]{0:T(1024)S(1)} %negate_bitcast_fusion.1), kind=kLoop, calls=%fused_computation.4 | loop fusion | flops 3144704 | bytes 4206592 | tf_op jit(solution)/shard_map/reduce_sum | solution.py:50
  111.4 14.2 %all_to_all.51 = f32[32,8,128]{2,1,0:T(8,128)S(1)} all-to-all(f32[32,8,128]{2,1,0:T(8,128)S(1)} %broadcast_in_dim.26), channel_id=1, replica_groups=mesh['src'=16,'tgt'=32] {'tgt'}, dimensions={0} | all-to-all | bytes 262144 | tf_op jit(solution)/shard_map/all_to_all | solution.py:13
  125.6 3.1 %exponential_reduce_fusion.2 = f32[1024]{0:T(1024)S(1)} fusion(f32[1024,1024]{0,1:T(8,128)} %copy-done, f32[1024]{0:T(1024)S(1)} %bitcast_subtract_fusion.3, f32[1024]{0:T(1024)S(1)} %negate_bitcast_fusion), kind=kLoop, calls=%fused_computation.3 | loop fusion | flops 3144704 | bytes 4206592 | tf_op jit(solution)/shard_map/reduce_sum | solution.py:52
  128.7 10.5 %all_to_all.52 = f32[16,8,128]{2,1,0:T(8,128)S(1)} all-to-all(f32[16,8,128]{2,1,0:T(8,128)S(1)} %broadcast_in_dim.28), channel_id=1, replica_groups=mesh['src'=16,'tgt'=32] {'src'}, dimensions={0} | all-to-all | bytes 131072 | tf_op jit(solution)/shard_map/all_to_all | solution.py:13
  139.2 2.9 %exponential_reduce_fusion.1 = f32[1024]{0:T(1024)S(1)} fusion(f32[1024,1024]{0,1:T(8,128)} %copy-done, f32[1024]{0:T(1024)S(1)} %bitcast_subtract_fusion.2, f32[1024]{0:T(1024)S(1)} %bitcast_subtract_fusion.3), kind=kLoop, calls=%fused_computation.2 | loop fusion | flops 3144704 | bytes 4206592 | tf_op jit(solution)/shard_map/reduce_sum | solution.py:50
  142.2 14.2 %all_to_all.53 = f32[32,8,128]{2,1,0:T(8,128)S(1)} all-to-all(f32[32,8,128]{2,1,0:T(8,128)S(1)} %broadcast_in_dim.30), channel_id=1, replica_groups=mesh['src'=16,'tgt'=32] {'tgt'}, dimensions={0} | all-to-all | bytes 262144 | tf_op jit(solution)/shard_map/all_to_all | solution.py:13
  156.5 3.2 %exponential_reduce_fusion = f32[1024]{0:T(1024)S(1)} fusion(f32[1024,1024]{0,1:T(8,128)} %copy-done, f32[1024]{0:T(1024)S(1)} %bitcast_subtract_fusion.1, f32[1024]{0:T(1024)S(1)} %bitcast_subtract_fusion.2), kind=kLoop, calls=%fused_computation.1 | loop fusion | flops 3144704 | bytes 4206592 | tf_op jit(solution)/shard_map/reduce_sum | solution.py:52
  159.7 10.5 %all_to_all.54 = f32[16,8,128]{2,1,0:T(8,128)S(1)} all-to-all(f32[16,8,128]{2,1,0:T(8,128)S(1)} %broadcast_in_dim.32), channel_id=1, replica_groups=mesh['src'=16,'tgt'=32] {'src'}, dimensions={0} | all-to-all | bytes 131072 | tf_op jit(solution)/shard_map/all_to_all | solution.py:13
  170.8 2.9 %fusion = f32[1024]{0:T(1024)S(1)} fusion(f32[1024,1024]{0,1:T(8,128)} %copy-done, f32[1024]{0:T(1024)S(1)} %get-tuple-element.3, f32[1024]{0:T(1024)S(1)} %bitcast_subtract_fusion.1), kind=kLoop, calls=%fused_computation.9 | loop fusion | flops 3144704 | bytes 4206592 | tf_op jit(solution)/shard_map/reduce_sum | solution.py:55
  174.5 4.0 %all-to-all-start.8 = ((f32[32,1,32]{2,1,0:T(1,128)}), f32[32,1,32]{2,1,0:T(1,128)S(1)}, u32[]{:S(2)}, u32[]{:S(2)}) async-start(f32[32,1,32]{2,1,0:T(1,128)} %all_to_all.38), calls=%async_computation.8 | async-start | bytes 32768 | tf_op jit(solution)/shard_map/all_to_all | solution.py:61
  178.5 16.3 %fusion.1 = f32[1024,384]{1,0:T(8,128)} fusion(f32[1024,384]{0,1:T(8,128)S(1)} %copy-done.2, f32[1024,1024]{0,1:T(8,128)} %copy-done, f32[1024]{0:T(1024)S(1)} %get-tuple-element.3, f32[1024]{0:T(1024)S(1)} %bitcast_subtract_fusion.1), kind=kOutput, calls=%fused_computation.10 | convolution fusion | flops 4833935360 | bytes 7348224 | tf_op jit(solution)/shard_map/dot_general | solution.py:56
  194.9 9.7 %all-to-all-start.7 = ((f32[32,32,384]{2,1,0:T(8,128)}), f32[32,32,384]{2,1,0:T(8,128)S(1)}, u32[]{:S(2)}, u32[]{:S(2)}) async-start(f32[32,32,384]{2,1,0:T(8,128)} %bitcast.13), calls=%async_computation.7 | async-start | bytes 3145728 | tf_op jit(solution)/shard_map/all_to_all | solution.py:60
  204.6 39.4 %all-to-all-done.7 = f32[32,32,384]{2,1,0:T(8,128)S(1)} async-done(((f32[32,32,384]{2,1,0:T(8,128)}), f32[32,32,384]{2,1,0:T(8,128)S(1)}, u32[]{:S(2)}, u32[]{:S(2)}) %all-to-all-start.7) | async-done | bytes 1572896 | tf_op jit(solution)/shard_map/all_to_all | solution.py:60
  (39 shorter events, 4.8 us)
Async XLA Ops:
  7.2 48.4 %all-gather.2.cloned.1.call-start = ((), (), s32[]{:S(2)}) async-start(), calls=%async_computation.9 | async-start | bytes 1671168 | tf_op jit(solution)/shard_map/all_gather | solution.py:29
  10.0 52.5 %all-to-all-start = ((f32[32,32,384]{2,1,0:T(8,128)}), f32[32,32,384]{2,1,0:T(8,128)S(1)}, u32[]{:S(2)}, u32[]{:S(2)}) async-start(f32[32,32,384]{2,1,0:T(8,128)} %broadcast_in_dim.22), calls=%async_computation | async-start | bytes 3145728 | tf_op jit(solution)/shard_map/all_to_all | solution.py:13
  71.7 1.9 copy-start
  90.1 3.4 %copy-start.1 = (f32[1024,1024]{0,1:T(8,128)S(1)}, f32[1024,1024]{0,1:T(8,128)}, u32[]{:S(2)}) copy-start(f32[1024,1024]{0,1:T(8,128)} %copy-done) | copy-start | bytes 12582916
  156.5 22.0 %copy-start.2 = (f32[1024,384]{0,1:T(8,128)S(1)}, f32[1024,384]{0,1:T(8,128)}, u32[]{:S(2)}) copy-start(f32[1024,384]{0,1:T(8,128)} %all-gather.2.cloned.1.call-done) | copy-start | bytes 4718596
  174.5 20.4 %all-to-all-start.8 = ((f32[32,1,32]{2,1,0:T(1,128)}), f32[32,1,32]{2,1,0:T(1,128)S(1)}, u32[]{:S(2)}, u32[]{:S(2)}) async-start(f32[32,1,32]{2,1,0:T(1,128)} %all_to_all.38), calls=%async_computation.8 | async-start | bytes 32768 | tf_op jit(solution)/shard_map/all_to_all | solution.py:61
  194.9 49.3 %copy-start.3 = (f32[32,384]{1,0:T(8,128)S(1)}, f32[32,384]{1,0:T(8,128)}, u32[]{:S(2)}) copy-start(f32[32,384]{1,0:T(8,128)} %param.2) | copy-start | bytes 147460
  194.9 49.2 %all-to-all-start.7 = ((f32[32,32,384]{2,1,0:T(8,128)}), f32[32,32,384]{2,1,0:T(8,128)S(1)}, u32[]{:S(2)}, u32[]{:S(2)}) async-start(f32[32,32,384]{2,1,0:T(8,128)} %bitcast.13), calls=%async_computation.7 | async-start | bytes 3145728 | tf_op jit(solution)/shard_map/all_to_all | solution.py:60
Sparse Core Ops, SparseCore 0:
  10.1 45.4 all-gather.1
where the time goes:
time: 253 us; the launch traced here: 252 us
  blocking collectives  79.1 us (31%)
  waiting for transfers between devices  77.9 us (31%)
  starting transfers between devices  27 us (11%)
  matrix products  25.2 us (10%)
  other arithmetic  22.7 us (9%)
  between operations  14.2 us (6%)
  local copies, waits for them, and re-layouts  5.58 us (2%)
    all_to_all x6, blocking collectives, spread(): lax.all_to_all(jnp.broadcast_to(value[None], (count,) + value.shape), axi...  79.1 us
    all_to_all x1, waiting for transfers between devices, per_device(): lax.all_to_all(part.reshape(count, own_rows, feat_width), 'tgt', 0, 0)  39.4 us
    all_gather x1, waiting for transfers between devices, per_device(): target_rows = lax.all_gather(data, 'src', axis=1, tiled=True)  32.4 us
    dot_general x1, matrix products, per_device(): jnp.dot(plan, target_rows, precision=lax.Precision.HIGHEST, preferred_ele...  16.3 us
    all_to_all x1, starting transfers between devices, spread(): lax.all_to_all(jnp.broadcast_to(value[None], (count,) + value.shape), axi...  13.2 us
    all_to_all x1, starting transfers between devices, per_device(): lax.all_to_all(part.reshape(count, own_rows, feat_width), 'tgt', 0, 0)  9.7 us
    dot_general x1, matrix products, per_device(): jnp.dot(source_rows, target_rows.T, precision=lax.Precision.HIGHEST, pref...  8.88 us
    reduce_sum x2, other arithmetic, per_device(): mass = jnp.sum(jnp.exp(f_pot[:, None] + gain + g_pot[None, :]), axis=0)  6.26 us
  transfers between devices with their start and end apart: 4, of which 3 were waited for; matrix products, arithmetic and copies ran while one was open for 8% of the time, Pallas kernels for 0%

commit v1 on v0

--- a/solution.py
+++ b/solution.py
@@ -3,9 +3,16 @@
 import jax.numpy as jnp
 from jax import lax
 from jax.sharding import PartitionSpec as P
+from jax.lax import all_to_all, axis_size
 
 ITERS = 3
 EPS = 0.05
+
+
+def divide_weights(which_axis, axis_no, v0):
+    high = jnp.stack(axis_size(which_axis) * [v0])
+    lower = all_to_all(high, axis_name=which_axis, split_axis=0, concat_axis=0)
+    return jnp.concatenate(lower, axis=axis_no)
 
 
 def spread(value, axis):
@@ -26,7 +33,7 @@
 
 
 def per_device(noise, data):
-    target_rows = lax.all_gather(data, "src", axis=1, tiled=True)
+    target_rows = divide_weights("src", 1, data)
     own_rows, feat_width = noise.shape
     source_rows = spread(noise, "tgt").reshape(-1, feat_width)
     src_total = source_rows.shape[0] * lax.axis_size("src")

time: 253 us -> 276 us (1.091)
  blocking collectives: 79.1 us -> 123 us
  between operations: 14.2 us -> 0.81 us
  matrix products: 25.2 us -> 17 us
    all_to_all x0 -> x1, blocking collectives: none -> 44.9 us  [divide_weights(): lower = all_to_all(high, axis_name=which_axis, split_axis=0, concat_axis=0)]
    all_to_all x1, waiting for transfers between devices: 5.41 us -> 39.7 us  [spread(): lax.all_to_all(jnp.broadcast_to(value[None], (count,) + value.shape), axi...]
    all_gather x1 -> x0, waiting for transfers between devices: 32.4 us -> none  [per_device(): target_rows = lax.all_gather(data, 'src', axis=1, tiled=True)]
    dot_general x1, matrix products: 16.3 us -> 9.53 us  [per_device(): jnp.dot(plan, target_rows, precision=lax.Precision.HIGHEST, preferred_ele...]
  transfers between devices with their start and end apart: 4 -> 3, of which waited for: 3 -> 3; matrix products, arithmetic and copies ran while one was open for 8% -> 4% of each run, Pallas kernels for 0% -> 0%
where the time goes in v1:
time: 276 us; the launch traced here: 275 us
  blocking collectives  123 us (45%)
  waiting for transfers between devices  79.3 us (29%)
  starting transfers between devices  25.7 us (9%)
  other arithmetic  23.6 us (9%)
  matrix products  17 us (6%)
  local copies, waits for them, and re-layouts  5.9 us (2%)
    all_to_all x6, blocking collectives, spread(): lax.all_to_all(jnp.broadcast_to(value[None], (count,) + value.shape), axi...  77.6 us
    all_to_all x1, blocking collectives, divide_weights(): lower = all_to_all(high, axis_name=which_axis, split_axis=0, concat_axis=0)  44.9 us
    all_to_all x1, waiting for transfers between devices, spread(): lax.all_to_all(jnp.broadcast_to(value[None], (count,) + value.shape), axi...  39.7 us
    all_to_all x1, waiting for transfers between devices, per_device(): lax.all_to_all(part.reshape(count, own_rows, feat_width), 'tgt', 0, 0)  39.4 us
    all_to_all x1, starting transfers between devices, spread(): lax.all_to_all(jnp.broadcast_to(value[None], (count,) + value.shape), axi...  12.3 us
    all_to_all x1, starting transfers between devices, per_device(): lax.all_to_all(part.reshape(count, own_rows, feat_width), 'tgt', 0, 0)  9.58 us
    dot_general x1, matrix products, per_device(): jnp.dot(plan, target_rows, precision=lax.Precision.HIGHEST, preferred_ele...  9.53 us
    dot_general x1, matrix products, per_device(): jnp.dot(source_rows, target_rows.T, precision=lax.Precision.HIGHEST, pref...  7.47 us
  transfers between devices with their start and end apart: 3, of which 3 were waited for; matrix products, arithmetic and copies ran while one was open for 4% of the time, Pallas kernels for 0%

profile of v1, /device:TPU:8, one launch (start us, length us, event | category | flops | bytes accessed | tf_op | source)
XLA Modules:
  0.0 274.8 jit_solution(12714504499150397524)
XLA Ops:
  0.6 1.1 stack.2
  1.7 44.9 %all_to_all.54 = f32[16,1024,24]{1,2,0:T(8,128)S(1)} all-to-all(f32[16,1024,24]{1,2,0:T(8,128)S(1)} %stack.2), channel_id=1, replica_groups=mesh['src'=16,'tgt'=32] {'src'}, dimensions={0} | all-to-all | bytes 3145728 | tf_op jit(solution)/shard_map/all_to_all | solution.py:14
  46.7 1.3 broadcast_in_dim.22
  48.0 12.3 %all-to-all-start = ((f32[32,32,384]{2,1,0:T(8,128)}), f32[32,32,384]{2,1,0:T(8,128)S(1)}, u32[]{:S(2)}, u32[]{:S(2)}) async-start(f32[32,32,384]{2,1,0:T(8,128)} %broadcast_in_dim.22), calls=%async_computation | async-start | bytes 3145728 | tf_op jit(solution)/shard_map/all_to_all | solution.py:20
  60.4 39.7 %all-to-all-done = f32[32,32,384]{2,1,0:T(8,128)S(1)} async-done(((f32[32,32,384]{2,1,0:T(8,128)}), f32[32,32,384]{2,1,0:T(8,128)S(1)}, u32[]{:S(2)}, u32[]{:S(2)}) %all-to-all-start) | async-done | bytes 1572896 | tf_op jit(solution)/shard_map/all_to_all | solution.py:20
  100.4 7.5 %fusion.2 = (f32[1024]{0:T(1024)S(1)}, f32[1024,1024]{1,0:T(8,128)S(1)}) fusion(f32[1024]{0:T(1024)S(1)} %fusion, f32[1024]{0:T(1024)S(1)} %sub.87, f32[1024,384]{1,0:T(8,128)S(1)} %bitcast.39, f32[1024,384]{0,1:T(8,128)S(1)} %bitcast.37), kind=kOutput, calls=%fused_computation.25 | convolution fusion | flops 4837080064 | bytes 7352320 | tf_op jit(solution)/shard_map/dot_general | solution.py:43
  107.9 2.0 copy-done
  109.8 1.1 exponential_reduce_fusion.5
  110.9 15.9 %all_to_all.55 = f32[32,8,128]{2,1,0:T(8,128)S(1)} all-to-all(f32[32,8,128]{2,1,0:T(8,128)S(1)} %broadcast_in_dim.23), channel_id=1, replica_groups=mesh['src'=16,'tgt'=32] {'tgt'}, dimensions={0} | all-to-all | bytes 262144 | tf_op jit(solution)/shard_map/all_to_all | solution.py:20
  126.9 2.7 add_reduce_fusion
  131.1 12.2 %all_to_all.56 = f32[16,8,128]{2,1,0:T(8,128)S(1)} all-to-all(f32[16,8,128]{2,1,0:T(8,128)S(1)} %broadcast_in_dim.24), channel_id=1, replica_groups=mesh['src'=16,'tgt'=32] {'src'}, dimensions={0} | all-to-all | bytes 131072 | tf_op jit(solution)/shard_map/all_to_all | solution.py:20
  143.4 3.1 %exponential_reduce_fusion.3 = f32[1024]{0:T(1024)S(1)} fusion(f32[1024,1024]{1,0:T(8,128)} %copy-done, f32[1024]{0:T(1024)S(1)} %negate_bitcast_fusion, f32[1024]{0:T(1024)S(1)} %negate_bitcast_fusion.1), kind=kLoop, calls=%fused_computation.4 | loop fusion | flops 3144704 | bytes 4206592 | tf_op jit(solution)/shard_map/reduce_sum | solution.py:57
  146.5 14.2 %all_to_all.57 = f32[32,8,128]{2,1,0:T(8,128)S(1)} all-to-all(f32[32,8,128]{2,1,0:T(8,128)S(1)} %broadcast_in_dim.26), channel_id=1, replica_groups=mesh['src'=16,'tgt'=32] {'tgt'}, dimensions={0} | all-to-all | bytes 262144 | tf_op jit(solution)/shard_map/all_to_all | solution.py:20
  160.8 3.0 %exponential_reduce_fusion.2 = f32[1024]{0:T(1024)S(1)} fusion(f32[1024,1024]{1,0:T(8,128)} %copy-done, f32[1024]{0:T(1024)S(1)} %bitcast_subtract_fusion.3, f32[1024]{0:T(1024)S(1)} %negate_bitcast_fusion), kind=kLoop, calls=%fused_computation.3 | loop fusion | flops 3144704 | bytes 4206592 | tf_op jit(solution)/shard_map/reduce_sum | solution.py:59
  163.8 10.5 %all_to_all.58 = f32[16,8,128]{2,1,0:T(8,128)S(1)} all-to-all(f32[16,8,128]{2,1,0:T(8,128)S(1)} %broadcast_in_dim.28), channel_id=1, replica_groups=mesh['src'=16,'tgt'=32] {'src'}, dimensions={0} | all-to-all | bytes 131072 | tf_op jit(solution)/shard_map/all_to_all | solution.py:20
  174.3 3.1 %exponential_reduce_fusion.1 = f32[1024]{0:T(1024)S(1)} fusion(f32[1024,1024]{1,0:T(8,128)} %copy-done, f32[1024]{0:T(1024)S(1)} %bitcast_subtract_fusion.2, f32[1024]{0:T(1024)S(1)} %bitcast_subtract_fusion.3), kind=kLoop, calls=%fused_computation.2 | loop fusion | flops 3144704 | bytes 4206592 | tf_op jit(solution)/shard_map/reduce_sum | solution.py:57
  177.4 14.2 %all_to_all.59 = f32[32,8,128]{2,1,0:T(8,128)S(1)} all-to-all(f32[32,8,128]{2,1,0:T(8,128)S(1)} %broadcast_in_dim.30), channel_id=1, replica_groups=mesh['src'=16,'tgt'=32] {'tgt'}, dimensions={0} | all-to-all | bytes 262144 | tf_op jit(solution)/shard_map/all_to_all | solution.py:20
  191.7 2.9 %exponential_reduce_fusion = f32[1024]{0:T(1024)S(1)} fusion(f32[1024,1024]{1,0:T(8,128)} %copy-done, f32[1024]{0:T(1024)S(1)} %bitcast_subtract_fusion.1, f32[1024]{0:T(1024)S(1)} %bitcast_subtract_fusion.2), kind=kLoop, calls=%fused_computation.1 | loop fusion | flops 3144704 | bytes 4206592 | tf_op jit(solution)/shard_map/reduce_sum | solution.py:59
  194.7 10.5 %all_to_all.60 = f32[16,8,128]{2,1,0:T(8,128)S(1)} all-to-all(f32[16,8,128]{2,1,0:T(8,128)S(1)} %broadcast_in_dim.32), channel_id=1, replica_groups=mesh['src'=16,'tgt'=32] {'src'}, dimensions={0} | all-to-all | bytes 131072 | tf_op jit(solution)/shard_map/all_to_all | solution.py:20
  205.8 4.9 %fusion.1 = (f32[1024]{0:T(1024)S(1)}, f32[1024,1024]{1,0:T(8,128)}) fusion(f32[1024]{0:T(1024)S(1)} %get-tuple-element.3, f32[1024,1024]{1,0:T(8,128)} %copy-done, f32[1024]{0:T(1024)S(1)} %bitcast_subtract_fusion.1), kind=kLoop, calls=%fused_computation.24 | loop fusion | flops 3144704 | bytes 8400896 | tf_op jit(solution)/shard_map/reduce_sum | solution.py:62
  211.4 3.8 %all-to-all-start.9 = ((f32[32,1,32]{2,1,0:T(1,128)}), f32[32,1,32]{2,1,0:T(1,128)S(1)}, u32[]{:S(2)}, u32[]{:S(2)}) async-start(f32[32,1,32]{2,1,0:T(1,128)} %all_to_all.42), calls=%async_computation.9 | async-start | bytes 32768 | tf_op jit(solution)/shard_map/all_to_all | solution.py:68
  215.3 9.5 %fusion.3 = f32[32,32,384]{2,1,0:T(8,128)} fusion(f32[32,32,1024]{2,1,0:T(8,128)} %bitcast.36, f32[1024,384,1]{0,1,2:T(8,128)S(1)} %bitcast.38), kind=kOutput, calls=%fused_computation.26 | convolution fusion | flops 4831838208 | bytes 7340032 | tf_op jit(solution)/shard_map/dot_general | solution.py:63
  225.0 9.6 %all-to-all-start.8 = ((f32[32,32,384]{2,1,0:T(8,128)}), f32[32,32,384]{2,1,0:T(8,128)S(1)}, u32[]{:S(2)}, u32[]{:S(2)}) async-start(f32[32,32,384]{2,1,0:T(8,128)} %fusion.3), calls=%async_computation.8 | async-start | bytes 3145728 | tf_op jit(solution)/shard_map/all_to_all | solution.py:67
  234.6 39.4 %all-to-all-done.8 = f32[32,32,384]{2,1,0:T(8,128)S(1)} async-done(((f32[32,32,384]{2,1,0:T(8,128)}), f32[32,32,384]{2,1,0:T(8,128)S(1)}, u32[]{:S(2)}, u32[]{:S(2)}) %all-to-all-start.8) | async-done | bytes 1572896 | tf_op jit(solution)/shard_map/all_to_all | solution.py:67
  (36 shorter events, 4.5 us)
Async XLA Ops:
  0.6 46.0 %copy-start.2 = (f32[32,384]{1,0:T(8,128)S(1)}, f32[32,384]{1,0:T(8,128)}, u32[]{:S(2)}) copy-start(f32[32,384]{1,0:T(8,128)} %param.2) | copy-start | bytes 147460
  48.0 52.1 %all-to-all-start = ((f32[32,32,384]{2,1,0:T(8,128)}), f32[32,32,384]{2,1,0:T(8,128)S(1)}, u32[]{:S(2)}, u32[]{:S(2)}) async-start(f32[32,32,384]{2,1,0:T(8,128)} %broadcast_in_dim.22), calls=%async_computation | async-start | bytes 3145728 | tf_op jit(solution)/shard_map/all_to_all | solution.py:20
  107.9 2.0 copy-start
  126.8 3.4 %copy-start.1 = (f32[1024,1024]{1,0:T(8,128)S(1)}, f32[1024,1024]{1,0:T(8,128)}, u32[]{:S(2)}) copy-start(f32[1024,1024]{1,0:T(8,128)} %copy-done) | copy-start | bytes 12582916
  211.4 13.6 %all-to-all-start.9 = ((f32[32,1,32]{2,1,0:T(1,128)}), f32[32,1,32]{2,1,0:T(1,128)S(1)}, u32[]{:S(2)}, u32[]{:S(2)}) async-start(f32[32,1,32]{2,1,0:T(1,128)} %all_to_all.42), calls=%async_computation.9 | async-start | bytes 32768 | tf_op jit(solution)/shard_map/all_to_all | solution.py:68
  225.0 49.0 %all-to-all-start.8 = ((f32[32,32,384]{2,1,0:T(8,128)}), f32[32,32,384]{2,1,0:T(8,128)S(1)}, u32[]{:S(2)}, u32[]{:S(2)}) async-start(f32[32,32,384]{2,1,0:T(8,128)} %fusion.3), calls=%async_computation.8 | async-start | bytes 3145728 | tf_op jit(solution)/shard_map/all_to_all | solution.py:67
